TPU v7x, 128 devices: a whole 4x4x4 slice. The times are simulated.
128 devices in a mesh: dp: 16 (over z, y_hi, core), seq: 8 (over x, y_lo).
Axes of the slice: x: 4, y: 4 (y_hi: 2, y_lo: 2; y = y_hi * 2 + y_lo), z: 4, core: 2. Of those that a mesh axis runs over, the one named last changes fastest.
Arguments:
- streams: bfloat16 [3, 16, 2048, 512], P(None, 'dp', 'seq'), may hold values from -6 to 6
- short_filter: float32 [3, 3, 512], replicated, may hold values from -3 to 3
- long_filter: float32 [2048, 512], P('seq'), may hold values from -4 to 4
- skip_gain: float32 [512], replicated, may hold values from -4 to 4
- out_weight: bfloat16 [512, 4096], replicated, may hold values from -0.25 to 0.25
- out_grad: bfloat16 [16, 2048, 4096], P('dp', 'seq'), may hold values from -6 to 6
Outputs:
- layer_out: bfloat16 [16, 2048, 4096], P('dp', 'seq')
- grad_streams: bfloat16 [3, 16, 2048, 512], P(None, 'dp', 'seq')
- grad_filter: float32 [2048, 512], P('seq')
- grad_out_weight: float32 [512, 4096], replicated
All inputs are finite; a program needn't handle non-finite values.
Results may differ from a plain program's by a relative error of at most 0.0049.
Values may be sent and summed in bfloat16 or wider, within the bound.
No kernel may reach another device: no remote copies, remote signals or barrier semaphores. Data moves between devices by JAX's collectives and lax.ppermute only.
A program may use at most 128 MiB of HBM per device.

v0:
```python
import math
import jax
import jax.numpy as jnp
from jax import lax
from jax.sharding import PartitionSpec as P


def swapped(array, axis, apart):
    return lax.ppermute(array, axis, [(i, i ^ 1 << apart) for i in range(lax.axis_size(axis))])


def passed_along(block, axis, distance):
    devices = range(lax.axis_size(axis))
    route = [(i - distance, i) for i in devices if i - distance in devices]
    return lax.ppermute(block, axis, route)


def spectral_table(length_here):
    row_index = lax.broadcasted_iota(jnp.int32, (length_here, length_here), 0)
    col_index = lax.broadcasted_iota(jnp.int32, (length_here, length_here), 1)
    phase_angle = (row_index * col_index % length_here).astype(jnp.float32) * (
        2.0 * math.pi / length_here
    )
    return (jnp.cos(phase_angle), jnp.sin(phase_angle))


def table_apply(matrix, values, pattern):
    return jnp.einsum(pattern, matrix, values, precision=lax.Precision.HIGHEST)


def transform_along(real_part, imaginary, direction, pattern):
    cosine, sine_table = spectral_table(real_part.shape[1])
    cosine_real = table_apply(cosine, real_part, pattern)
    cosine_imaginary = table_apply(cosine, imaginary, pattern)
    sine_real = table_apply(sine_table, real_part, pattern)
    sine_imaginary = table_apply(sine_table, imaginary, pattern)
    return (cosine_real - direction * sine_imaginary, cosine_imaginary + direction * sine_real)


def rotate_complex(real_part, imaginary, cosine, sine_value):
    return (
        real_part * cosine - imaginary * sine_value,
        real_part * sine_value + imaginary * cosine,
    )


def branch_angle(start_row, block_rows, total_length):
    positions = start_row + lax.broadcasted_iota(jnp.int32, (1, block_rows, 1), 1)
    return positions.astype(jnp.float32) * (math.pi / total_length)


def padded_branches(signal, start_row, total_length):
    phase_angle = branch_angle(start_row, signal.shape[1], total_length)
    real_part = jnp.concatenate([signal, signal * jnp.cos(phase_angle)], axis=0)
    imaginary = jnp.concatenate([jnp.zeros_like(signal), -signal * jnp.sin(phase_angle)], axis=0)
    return (real_part, imaginary)


def combine_branches(real_part, imaginary, start_row, total_length):
    members = real_part.shape[0] // 2
    phase_angle = branch_angle(start_row, real_part.shape[1], total_length)
    return 0.5 * (
        real_part[:members]
        + jnp.cos(phase_angle) * real_part[members:]
        - jnp.sin(phase_angle) * imaginary[members:]
    )


def level_twiddle(position, split_bit, block_rows):
    half_span = block_rows * (1 << split_bit)
    within = position % (1 << split_bit) * block_rows + lax.broadcasted_iota(
        jnp.int32, (1, block_rows, 1), 1
    )
    phase_angle = within.astype(jnp.float32) * (math.pi / half_span)
    return (jnp.cos(phase_angle), -jnp.sin(phase_angle))


def forward_levels(real_part, imaginary):
    seq_count = lax.axis_size("seq")
    position = lax.axis_index("seq")
    block_rows = real_part.shape[1]
    for split_bit in reversed(range(seq_count.bit_length() - 1)):
        upper_half = position >> split_bit & 1 == 1
        cosine, sine_value = level_twiddle(position, split_bit, block_rows)
        other_real, other_imaginary = swapped((real_part, imaginary), "seq", split_bit)
        turned_real, turned_imaginary = rotate_complex(
            other_real - real_part, other_imaginary - imaginary, cosine, sine_value
        )
        real_part = jnp.where(upper_half, turned_real, real_part + other_real)
        imaginary = jnp.where(upper_half, turned_imaginary, imaginary + other_imaginary)
    return (real_part, imaginary)


def inverse_levels(real_part, imaginary):
    seq_count = lax.axis_size("seq")
    position = lax.axis_index("seq")
    block_rows = real_part.shape[1]
    for split_bit in range(seq_count.bit_length() - 1):
        upper_half = position >> split_bit & 1 == 1
        cosine, sine_value = level_twiddle(position, split_bit, block_rows)
        turned_real, turned_imaginary = rotate_complex(real_part, imaginary, cosine, -sine_value)
        own_real = jnp.where(upper_half, turned_real, real_part)
        own_imaginary = jnp.where(upper_half, turned_imaginary, imaginary)
        other_real, other_imaginary = swapped((own_real, own_imaginary), "seq", split_bit)
        real_part = 0.5 * jnp.where(upper_half, other_real - own_real, other_real + own_real)
        imaginary = 0.5 * jnp.where(
            upper_half, other_imaginary - own_imaginary, other_imaginary + own_imaginary
        )
    return (real_part, imaginary)


def forward_spectrum(signal, start_row, total_length):
    real_part, imaginary = padded_branches(signal, start_row, total_length)
    real_part, imaginary = forward_levels(real_part, imaginary)
    return transform_along(real_part, imaginary, -1.0, "js,msc->mjc")


def inverse_signal(real_part, imaginary, start_row, total_length):
    block_rows = real_part.shape[1]
    real_part, imaginary = transform_along(real_part, imaginary, 1.0, "js,msc->mjc")
    real_part = real_part / block_rows
    imaginary = imaginary / block_rows
    real_part, imaginary = inverse_levels(real_part, imaginary)
    return combine_branches(real_part, imaginary, start_row, total_length)


def on_device(streams, short_filter, long_filter, skip_gain, out_weight, out_grad):
    seq_count = lax.axis_size("seq")
    batch_here = streams.shape[1]
    block_rows = streams.shape[2]
    channels = streams.shape[3]
    total_length = block_rows * seq_count
    start_row = lax.axis_index("seq") * block_rows
    grad_scale = 1.0 / math.sqrt(batch_here * lax.axis_size("dp") * total_length)
    earlier = passed_along(streams[:, :, block_rows - 2 :, :], "seq", 1)
    extended = jnp.concatenate([earlier, streams], axis=2).astype(jnp.float32)
    shortened = sum(
        (
            short_filter[:, offset, None, None, :]
            * extended[:, :, 2 - offset : 2 - offset + block_rows, :]
            for offset in range(3)
        )
    )
    gate_out, gate_in, value_stream = (shortened[0], shortened[1], shortened[2])
    product = gate_in * value_stream
    members = batch_here + 1
    spectrum_real, spectrum_imaginary = forward_spectrum(
        jnp.concatenate([product, long_filter[None]], axis=0), start_row, total_length
    )
    spectrum_real = spectrum_real.reshape(2, members, block_rows, channels)
    spectrum_imaginary = spectrum_imaginary.reshape(2, members, block_rows, channels)
    product_real, product_imaginary = (
        spectrum_real[:, :batch_here],
        spectrum_imaginary[:, :batch_here],
    )
    filter_real, filter_imaginary = (
        spectrum_real[:, batch_here:],
        spectrum_imaginary[:, batch_here:],
    )
    conv_real = product_real * filter_real - product_imaginary * filter_imaginary
    conv_imaginary = product_real * filter_imaginary + product_imaginary * filter_real
    convolved = inverse_signal(
        conv_real.reshape(2 * batch_here, block_rows, channels),
        conv_imaginary.reshape(2 * batch_here, block_rows, channels),
        start_row,
        total_length,
    )
    convolved = convolved + skip_gain * product
    mixed_out = (gate_out * convolved).astype(jnp.bfloat16)
    mixed_flat = mixed_out.reshape(batch_here * block_rows, channels)
    grad_flat = out_grad.reshape(batch_here * block_rows, out_grad.shape[2])
    layer_out = (
        jnp.dot(mixed_flat, out_weight, preferred_element_type=jnp.float32)
        .astype(jnp.bfloat16)
        .reshape(out_grad.shape)
    )
    grad_mixed = lax.dot_general(
        grad_flat, out_weight, (((1,), (1,)), ((), ())), preferred_element_type=jnp.float32
    ).reshape(batch_here, block_rows, channels)
    grad_conv = grad_mixed * gate_out
    grad_gate_out = grad_mixed * convolved
    grad_real, grad_imaginary = forward_spectrum(grad_conv, start_row, total_length)
    grad_real = grad_real.reshape(2, batch_here, block_rows, channels)
    grad_imaginary = grad_imaginary.reshape(2, batch_here, block_rows, channels)
    back_real = filter_real * grad_real + filter_imaginary * grad_imaginary
    back_imaginary = filter_real * grad_imaginary - filter_imaginary * grad_real
    lag_real = jnp.sum(
        product_real * grad_real + product_imaginary * grad_imaginary, axis=1, keepdims=True
    )
    lag_imaginary = jnp.sum(
        product_real * grad_imaginary - product_imaginary * grad_real, axis=1, keepdims=True
    )
    joined_real = jnp.concatenate([back_real, lag_real], axis=1).reshape(
        2 * members, block_rows, channels
    )
    joined_imaginary = jnp.concatenate([back_imaginary, lag_imaginary], axis=1).reshape(
        2 * members, block_rows, channels
    )
    inverse_rows = inverse_signal(joined_real, joined_imaginary, start_row, total_length)
    grad_product = inverse_rows[:batch_here] + skip_gain * grad_conv
    filter_part = inverse_rows[batch_here]
    grad_shortened = jnp.stack([grad_gate_out, grad_product * value_stream, grad_product * gate_in])
    later_rows = passed_along(grad_shortened[:, :, :2, :], "seq", -1)
    extended_grad = jnp.concatenate([grad_shortened, later_rows], axis=2)
    grad_streams = sum(
        (
            short_filter[:, offset, None, None, :]
            * extended_grad[:, :, offset : offset + block_rows, :]
            for offset in range(3)
        )
    )
    partial_value = lax.dot_general(
        mixed_flat, grad_flat, (((0,), (0,)), ((), ())), preferred_element_type=jnp.float32
    )
    grad_out_weight = lax.psum(partial_value, ("dp", "seq")) * grad_scale
    grad_filter = lax.psum(filter_part, "dp") * grad_scale
    return (layer_out, grad_streams.astype(jnp.bfloat16), grad_filter, grad_out_weight)


def solution(mesh):
    placed = (P(None, "dp", "seq", None), P(), P("seq", None), P(), P(), P("dp", "seq", None))
    return jax.shard_map(
        on_device,
        mesh=mesh,
        in_specs=placed,
        out_specs=(P("dp", "seq", None), P(None, "dp", "seq", None), P("seq", None), P()),
        check_vma=False,
    )
```

profile of v0, /device:TPU:1, one launch (start us, length us, event | category | flops | bytes accessed | tf_op | source)
XLA Modules:
  0.0 1175.4 jit_solution(6477687003662021271)
XLA Ops:
  8.1 4.0 collective-permute-start
  13.2 1.4 maximum_convert_fusion
  15.8 1.5 pad_maximum_fusion
  17.5 3.8 collective-permute-start.1
  21.3 1.6 concatenate.47
  26.8 2.6 collective-permute-start.13
  31.0 34.8 %collective-permute-done.1 = f32[4,256,512]{2,1,0:T(8,128)} collective-permute-done((f32[4,256,512]{2,1,0:T(8,128)}, f32[4,256,512]{2,1,0:T(8,128)}, u32[]{:S(2)}, u32[]{:S(2)}) %collective-permute-start.1) | collective-permute-done | bytes 2097184 | tf_op jit(solution)/shard_map/ppermute | solution.py:9
  65.7 44.9 %collective-permute-done.2 = f32[4,256,512]{2,1,0:T(8,128)} collective-permute-done((f32[4,256,512]{2,1,0:T(8,128)}, f32[4,256,512]{2,1,0:T(8,128)}, u32[]{:S(2)}, u32[]{:S(2)}) %collective-permute-start.2) | collective-permute-done | bytes 2097184 | tf_op jit(solution)/shard_map/ppermute | solution.py:9
  110.7 6.2 add_select_fusion.9
  118.4 14.8 %collective-permute-done.13 = f32[2,256,512]{2,1,0:T(8,128)} collective-permute-done((f32[2,256,512]{2,1,0:T(8,128)}, f32[2,256,512]{2,1,0:T(8,128)}, u32[]{:S(2)}, u32[]{:S(2)}) %collective-permute-start.13) | collective-permute-done | bytes 1048608 | tf_op jit(solution)/shard_map/ppermute | solution.py:9
  133.1 22.5 %collective-permute-done.14 = f32[2,256,512]{2,1,0:T(8,128)} collective-permute-done((f32[2,256,512]{2,1,0:T(8,128)}, f32[2,256,512]{2,1,0:T(8,128)}, u32[]{:S(2)}, u32[]{:S(2)}) %collective-permute-start.14) | collective-permute-done | bytes 1048608 | tf_op jit(solution)/shard_map/ppermute | solution.py:9
  155.6 3.5 add_select_fusion.14
  160.6 107.4 %collective-permute-done.15 = f32[2,256,512]{2,1,0:T(8,128)} collective-permute-done((f32[2,256,512]{2,1,0:T(8,128)}, f32[2,256,512]{2,1,0:T(8,128)}, u32[]{:S(2)}, u32[]{:S(2)}) %collective-permute-start.15) | collective-permute-done | bytes 1048608 | tf_op jit(solution)/shard_map/ppermute | solution.py:9
  268.0 22.5 %collective-permute-done.16 = f32[2,256,512]{2,1,0:T(8,128)} collective-permute-done((f32[2,256,512]{2,1,0:T(8,128)}, f32[2,256,512]{2,1,0:T(8,128)}, u32[]{:S(2)}, u32[]{:S(2)}) %collective-permute-start.16) | collective-permute-done | bytes 1048608 | tf_op jit(solution)/shard_map/ppermute | solution.py:9
  290.5 4.1 add_select_fusion.12
  296.1 6.7 add_select_fusion.7
  303.1 1.6 collective-permute-start.6
  304.8 12.0 %collective-permute-done.17 = f32[2,256,512]{2,1,0:T(8,128)} collective-permute-done((f32[2,256,512]{2,1,0:T(8,128)}, f32[2,256,512]{2,1,0:T(8,128)}, u32[]{:S(2)}, u32[]{:S(2)}) %collective-permute-start.17) | collective-permute-done | bytes 1048608 | tf_op jit(solution)/shard_map/ppermute | solution.py:9
  316.8 22.5 %collective-permute-done.18 = f32[2,256,512]{2,1,0:T(8,128)} collective-permute-done((f32[2,256,512]{2,1,0:T(8,128)}, f32[2,256,512]{2,1,0:T(8,128)}, u32[]{:S(2)}, u32[]{:S(2)}) %collective-permute-start.18) | collective-permute-done | bytes 1048608 | tf_op jit(solution)/shard_map/ppermute | solution.py:9
  339.3 2.7 add_select_fusion.10
  342.0 2.7 convolution_multiply_fusion
  344.7 2.7 fusion.10
  347.4 2.7 convolution_multiply_fusion.1
  350.0 34.2 %collective-permute-done.5 = f32[4,256,512]{2,1,0:T(8,128)} collective-permute-done((f32[4,256,512]{2,1,0:T(8,128)}, f32[4,256,512]{2,1,0:T(8,128)}, u32[]{:S(2)}, u32[]{:S(2)}) %collective-permute-start.5) | collective-permute-done | bytes 2097184 | tf_op jit(solution)/shard_map/ppermute | solution.py:9
  384.2 44.9 %collective-permute-done.6 = f32[4,256,512]{2,1,0:T(8,128)} collective-permute-done((f32[4,256,512]{2,1,0:T(8,128)}, f32[4,256,512]{2,1,0:T(8,128)}, u32[]{:S(2)}, u32[]{:S(2)}) %collective-permute-start.6) | collective-permute-done | bytes 2097184 | tf_op jit(solution)/shard_map/ppermute | solution.py:9
  429.2 4.6 add_select_fusion.5
  433.8 4.7 fusion.39
  438.5 4.5 fusion.41
  443.0 4.5 multiply_add_fusion
  447.5 4.9 multiply_subtract_fusion
  452.4 6.3 multiply_subtract_fusion.2
  458.7 1.5 pad_maximum_fusion.1
  460.2 2.9 copy.42
  463.1 3.0 pad_maximum_fusion.2
  466.1 2.9 copy.43
  469.0 4.8 fusion.43
  473.8 3.1 fusion.45
  476.9 3.3 convolution_add_fusion
  480.2 4.0 select_bitcast_fusion
  485.9 2.1 fusion.15
  488.0 2.1 fusion.19
  490.0 2.1 convolution_add_fusion.2
  492.1 35.7 %collective-permute-done.19 = f32[4,256,512]{2,1,0:T(8,128)S(1)} collective-permute-done((f32[4,256,512]{2,1,0:T(8,128)S(1)}, f32[4,256,512]{2,1,0:T(8,128)S(1)}, u32[]{:S(2)}, u32[]{:S(2)}) %collective-permute-start.19) | collective-permute-done | bytes 2097184 | tf_op jit(solution)/shard_map/ppermute | solution.py:9
  527.8 44.9 %collective-permute-done.20 = f32[4,256,512]{2,1,0:T(8,128)S(1)} collective-permute-done((f32[4,256,512]{2,1,0:T(8,128)S(1)}, f32[4,256,512]{2,1,0:T(8,128)S(1)}, u32[]{:S(2)}, u32[]{:S(2)}) %collective-permute-start.20) | collective-permute-done | bytes 2097184 | tf_op jit(solution)/shard_map/ppermute | solution.py:9
  572.7 1.5 multiply_select_fusion.2
  576.0 2.5 select_bitcast_fusion.2
  580.0 18.0 %collective-permute-done.7 = f32[2,256,512]{2,1,0:T(8,128)S(1)} collective-permute-done((f32[2,256,512]{2,1,0:T(8,128)S(1)}, f32[2,256,512]{2,1,0:T(8,128)S(1)}, u32[]{:S(2)}, u32[]{:S(2)}) %collective-permute-start.7) | collective-permute-done | bytes 1048608 | tf_op jit(solution)/shard_map/ppermute | solution.py:9
  598.0 22.5 %collective-permute-done.8 = f32[2,256,512]{2,1,0:T(8,128)S(1)} collective-permute-done((f32[2,256,512]{2,1,0:T(8,128)S(1)}, f32[2,256,512]{2,1,0:T(8,128)S(1)}, u32[]{:S(2)}, u32[]{:S(2)}) %collective-permute-start.8) | collective-permute-done | bytes 1048608 | tf_op jit(solution)/shard_map/ppermute | solution.py:9
  622.7 39.0 %collective-permute-done.22 = f32[4,256,512]{2,1,0:T(8,128)S(1)} collective-permute-done((f32[4,256,512]{2,1,0:T(8,128)S(1)}, f32[4,256,512]{2,1,0:T(8,128)S(1)}, u32[]{:S(2)}, u32[]{:S(2)}) %collective-permute-start.22) | collective-permute-done | bytes 2097184 | tf_op jit(solution)/shard_map/ppermute | solution.py:9
  661.8 1.5 multiply_select_fusion
  663.3 1.8 collective-permute-start.23
  666.3 17.9 %collective-permute-done.10 = f32[2,256,512]{2,1,0:T(8,128)S(1)} collective-permute-done((f32[2,256,512]{2,1,0:T(8,128)S(1)}, f32[2,256,512]{2,1,0:T(8,128)S(1)}, u32[]{:S(2)}, u32[]{:S(2)}) %collective-permute-start.10) | collective-permute-done | bytes 1048608 | tf_op jit(solution)/shard_map/ppermute | solution.py:9
  684.2 22.5 %collective-permute-done.9 = f32[2,256,512]{2,1,0:T(8,128)S(1)} collective-permute-done((f32[2,256,512]{2,1,0:T(8,128)S(1)}, f32[2,256,512]{2,1,0:T(8,128)S(1)}, u32[]{:S(2)}, u32[]{:S(2)}) %collective-permute-start.9) | collective-permute-done | bytes 1048608 | tf_op jit(solution)/shard_map/ppermute | solution.py:9
  707.4 1.8 collective-permute-start.11
  710.5 109.4 %collective-permute-done.11 = f32[2,256,512]{2,1,0:T(8,128)S(1)} collective-permute-done((f32[2,256,512]{2,1,0:T(8,128)S(1)}, f32[2,256,512]{2,1,0:T(8,128)S(1)}, u32[]{:S(2)}, u32[]{:S(2)}) %collective-permute-start.11) | collective-permute-done | bytes 1048608 | tf_op jit(solution)/shard_map/ppermute | solution.py:9
  820.2 22.2 %collective-permute-done.12 = f32[2,256,512]{2,1,0:T(8,128)S(1)} collective-permute-done((f32[2,256,512]{2,1,0:T(8,128)S(1)}, f32[2,256,512]{2,1,0:T(8,128)S(1)}, u32[]{:S(2)}, u32[]{:S(2)}) %collective-permute-start.12) | collective-permute-done | bytes 1048608 | tf_op jit(solution)/shard_map/ppermute | solution.py:9
  845.8 4.7 fusion.1
  852.8 1.7 collective-permute-start.25
  854.5 4.8 fusion
  859.4 1.4 fusion.6
  860.8 130.1 %all-reduce.5.cloned.1.call-done = f32[256,512]{1,0:T(8,128)} async-done(((f32[256,512]{1,0:T(8,128)}), f32[256,512]{1,0:T(8,128)}) %all-reduce.5.cloned.1.call-update) | async-done | bytes 524304 | tf_op jit(solution)/shard_map/psum | solution.py:216
  990.9 1.9 broadcast_multiply_fusion.1
  992.7 167.3 %all-reduce.7.cloned.1.call-done = f32[512,4096]{1,0:T(8,128)} async-done(((f32[512,4096]{1,0:T(8,128)}), f32[512,4096]{1,0:T(8,128)}) %all-reduce.7.cloned.1.call-update) | async-done | bytes 8388624 | tf_op jit(solution)/shard_map/psum | solution.py:215
  1160.1 8.3 broadcast_multiply_fusion
  (100 shorter events, 30.0 us)
Async XLA Ops:
  7.2 16.1 %copy-start = (bf16[1,256,4096]{2,1,0:T(8,128)(2,1)S(1)}, bf16[1,256,4096]{2,1,0:T(8,128)(2,1)}, u32[]{:S(2)}) copy-start(bf16[1,256,4096]{2,1,0:T(8,128)(2,1)} %param.11) | copy-start | bytes 6291460
  7.2 983.7 %all-reduce.5.cloned.1.call-start = ((), (), s32[]{:S(2)}) async-start(), calls=%async_computation | async-start | bytes 1048576 | tf_op jit(solution)/shard_map/psum | solution.py:216
  8.1 5.0 collective-permute-start
  14.5 1.0 copy-start.11
  15.0 9.6 copy-start.1
  15.8 1.7 copy-start.6
  15.8 5.5 copy-start.5
  15.8 7.5 copy-start.19
  17.5 48.2 %collective-permute-start.1 = (f32[4,256,512]{2,1,0:T(8,128)}, f32[4,256,512]{2,1,0:T(8,128)}, u32[]{:S(2)}, u32[]{:S(2)}) collective-permute-start(f32[4,256,512]{2,1,0:T(8,128)} %pad_maximum_fusion), channel_id=1, source_target_pairs={{0,4},{1,5},{2,6},{3,7},{4,0},{5,1},{6,2},{7,3},{8,12},{9,13},{10,... | collective-permute-start | bytes 6291464 | tf_op jit(solution)/shard_map/ppermute | solution.py:9
  22.9 87.8 %collective-permute-start.2 = (f32[4,256,512]{2,1,0:T(8,128)}, f32[4,256,512]{2,1,0:T(8,128)}, u32[]{:S(2)}, u32[]{:S(2)}) collective-permute-start(f32[4,256,512]{2,1,0:T(8,128)} %concatenate.47), channel_id=1, source_target_pairs={{0,4},{1,5},{2,6},{3,7},{4,0},{5,1},{6,2},{7,3},{8,12},{9,13},{10,... | collective-permute-start | bytes 6291464 | tf_op jit(solution)/shard_map/ppermute | solution.py:9
  24.6 2.2 copy-start.16
  24.7 5.8 copy-start.14
  24.9 0.9 copy-start.12
  26.8 106.3 %collective-permute-start.13 = (f32[2,256,512]{2,1,0:T(8,128)}, f32[2,256,512]{2,1,0:T(8,128)}, u32[]{:S(2)}, u32[]{:S(2)}) collective-permute-start(f32[2,256,512]{2,1,0:T(8,128)} %pad_maximum_fusion.6), channel_id=1, source_target_pairs={{0,4},{1,5},{2,6},{3,7},{4,0},{5,1},{6,2},{7,3},{8,12},{9,13},{10,... | collective-permute-start | bytes 3145736 | tf_op jit(solution)/shard_map/ppermute | solution.py:9
  30.5 125.1 %collective-permute-start.14 = (f32[2,256,512]{2,1,0:T(8,128)}, f32[2,256,512]{2,1,0:T(8,128)}, u32[]{:S(2)}, u32[]{:S(2)}) collective-permute-start(f32[2,256,512]{2,1,0:T(8,128)} %concatenate.49), channel_id=1, source_target_pairs={{0,4},{1,5},{2,6},{3,7},{4,0},{5,1},{6,2},{7,3},{8,12},{9,13},{10,... | collective-permute-start | bytes 3145736 | tf_op jit(solution)/shard_map/ppermute | solution.py:9
  110.7 44.9 %copy-start.13 = (f32[1,256,512]{2,1,0:T(8,128)S(1)}, f32[1,256,512]{2,1,0:T(8,128)}, u32[]{:S(2)}) copy-start(f32[1,256,512]{2,1,0:T(8,128)} %copy-done.12) | copy-start | bytes 1572868
  110.7 44.9 %copy-start.15 = (f32[1,256,512]{2,1,0:T(8,128)S(1)}, f32[1,256,512]{2,1,0:T(8,128)}, u32[]{:S(2)}) copy-start(f32[1,256,512]{2,1,0:T(8,128)} %copy-done.14) | copy-start | bytes 1572868
  116.9 179.2 %collective-permute-start.3 = (f32[4,256,512]{2,1,0:T(8,128)}, f32[4,256,512]{2,1,0:T(8,128)}, u32[]{:S(2)}, u32[]{:S(2)}) collective-permute-start(f32[4,256,512]{2,1,0:T(8,128)} %get-tuple-element.16), channel_id=1, source_target_pairs={{0,2},{1,3},{2,0},{3,1},{4,6},{5,7},{6,4},{7,5},{8,10},{9,11},{10,... | collective-permute-start | bytes 6291464 | tf_op jit(solution)/shard_map/ppermute | solution.py:9
  118.0 178.0 %collective-permute-start.4 = (f32[4,256,512]{2,1,0:T(8,128)}, f32[4,256,512]{2,1,0:T(8,128)}, u32[]{:S(2)}, u32[]{:S(2)}) collective-permute-start(f32[4,256,512]{2,1,0:T(8,128)} %get-tuple-element.17), channel_id=1, source_target_pairs={{0,2},{1,3},{2,0},{3,1},{4,6},{5,7},{6,4},{7,5},{8,10},{9,11},{10,... | collective-permute-start | bytes 6291464 | tf_op jit(solution)/shard_map/ppermute | solution.py:9
  159.1 108.9 %collective-permute-start.15 = (f32[2,256,512]{2,1,0:T(8,128)}, f32[2,256,512]{2,1,0:T(8,128)}, u32[]{:S(2)}, u32[]{:S(2)}) collective-permute-start(f32[2,256,512]{2,1,0:T(8,128)} %get-tuple-element.35), channel_id=1, source_target_pairs={{0,2},{1,3},{2,0},{3,1},{4,6},{5,7},{6,4},{7,5},{8,10},{9,11},{10,... | collective-permute-start | bytes 3145736 | tf_op jit(solution)/shard_map/ppermute | solution.py:9
  160.2 130.2 %collective-permute-start.16 = (f32[2,256,512]{2,1,0:T(8,128)}, f32[2,256,512]{2,1,0:T(8,128)}, u32[]{:S(2)}, u32[]{:S(2)}) collective-permute-start(f32[2,256,512]{2,1,0:T(8,128)} %get-tuple-element.34), channel_id=1, source_target_pairs={{0,2},{1,3},{2,0},{3,1},{4,6},{5,7},{6,4},{7,5},{8,10},{9,11},{10,... | collective-permute-start | bytes 3145736 | tf_op jit(solution)/shard_map/ppermute | solution.py:9
  294.6 22.2 %collective-permute-start.17 = (f32[2,256,512]{2,1,0:T(8,128)}, f32[2,256,512]{2,1,0:T(8,128)}, u32[]{:S(2)}, u32[]{:S(2)}) collective-permute-start(f32[2,256,512]{2,1,0:T(8,128)} %get-tuple-element.27), channel_id=1, source_target_pairs={{0,1},{1,0},{2,3},{3,2},{4,5},{5,4},{6,7},{7,6},{8,9},{9,8},{10,11... | collective-permute-start | bytes 3145736 | tf_op jit(solution)/shard_map/ppermute | solution.py:9
  295.0 44.3 %collective-permute-start.18 = (f32[2,256,512]{2,1,0:T(8,128)}, f32[2,256,512]{2,1,0:T(8,128)}, u32[]{:S(2)}, u32[]{:S(2)}) collective-permute-start(f32[2,256,512]{2,1,0:T(8,128)} %get-tuple-element.26), channel_id=1, source_target_pairs={{0,1},{1,0},{2,3},{3,2},{4,5},{5,4},{6,7},{7,6},{8,9},{9,8},{10,11... | collective-permute-start | bytes 3145736 | tf_op jit(solution)/shard_map/ppermute | solution.py:9
  302.7 81.5 %collective-permute-start.5 = (f32[4,256,512]{2,1,0:T(8,128)}, f32[4,256,512]{2,1,0:T(8,128)}, u32[]{:S(2)}, u32[]{:S(2)}) collective-permute-start(f32[4,256,512]{2,1,0:T(8,128)} %get-tuple-element.14), channel_id=1, source_target_pairs={{0,1},{1,0},{2,3},{3,2},{4,5},{5,4},{6,7},{7,6},{8,9},{9,8},{10,11... | collective-permute-start | bytes 6291464 | tf_op jit(solution)/shard_map/ppermute | solution.py:9
  303.1 126.0 %collective-permute-start.6 = (f32[4,256,512]{2,1,0:T(8,128)}, f32[4,256,512]{2,1,0:T(8,128)}, u32[]{:S(2)}, u32[]{:S(2)}) collective-permute-start(f32[4,256,512]{2,1,0:T(8,128)} %get-tuple-element.15), channel_id=1, source_target_pairs={{0,1},{1,0},{2,3},{3,2},{4,5},{5,4},{6,7},{7,6},{8,9},{9,8},{10,11... | collective-permute-start | bytes 6291464 | tf_op jit(solution)/shard_map/ppermute | solution.py:9
  469.0 4.8 copy-start.3
  476.9 3.3 copy-start.4
  480.2 5.6 copy-start.7
  484.3 3.7 copy-start.8
  484.3 43.5 %collective-permute-start.19 = (f32[4,256,512]{2,1,0:T(8,128)S(1)}, f32[4,256,512]{2,1,0:T(8,128)S(1)}, u32[]{:S(2)}, u32[]{:S(2)}) collective-permute-start(f32[4,256,512]{2,1,0:T(8,128)S(1)} %get-tuple-element.23), channel_id=1, source_target_pairs={{0,1},{1,0},{2,3},{3,2},{4,5},{5,4},{6,7},{7,6},{8,9},{9,8},{10,11... | collective-permute-start | bytes 6291464 | tf_op jit(solution)/shard_map/ppermute | solution.py:9
  484.7 88.0 %collective-permute-start.20 = (f32[4,256,512]{2,1,0:T(8,128)S(1)}, f32[4,256,512]{2,1,0:T(8,128)S(1)}, u32[]{:S(2)}, u32[]{:S(2)}) collective-permute-start(f32[4,256,512]{2,1,0:T(8,128)S(1)} %get-tuple-element.22), channel_id=1, source_target_pairs={{0,1},{1,0},{2,3},{3,2},{4,5},{5,4},{6,7},{7,6},{8,9},{9,8},{10,11... | collective-permute-start | bytes 6291464 | tf_op jit(solution)/shard_map/ppermute | solution.py:9
  574.2 48.5 %collective-permute-start.21 = (f32[4,256,512]{2,1,0:T(8,128)S(1)}, f32[4,256,512]{2,1,0:T(8,128)S(1)}, u32[]{:S(2)}, u32[]{:S(2)}) collective-permute-start(f32[4,256,512]{2,1,0:T(8,128)S(1)} %get-tuple-element.11), channel_id=1, source_target_pairs={{0,2},{1,3},{2,0},{3,1},{4,6},{5,7},{6,4},{7,5},{8,10},{9,11},{10,... | collective-permute-start | bytes 6291464 | tf_op jit(solution)/shard_map/ppermute | solution.py:9
  575.5 86.3 %collective-permute-start.22 = (f32[4,256,512]{2,1,0:T(8,128)S(1)}, f32[4,256,512]{2,1,0:T(8,128)S(1)}, u32[]{:S(2)}, u32[]{:S(2)}) collective-permute-start(f32[4,256,512]{2,1,0:T(8,128)S(1)} %get-tuple-element.10), channel_id=1, source_target_pairs={{0,2},{1,3},{2,0},{3,1},{4,6},{5,7},{6,4},{7,5},{8,10},{9,11},{10,... | collective-permute-start | bytes 6291464 | tf_op jit(solution)/shard_map/ppermute | solution.py:9
  578.4 19.6 %collective-permute-start.7 = (f32[2,256,512]{2,1,0:T(8,128)S(1)}, f32[2,256,512]{2,1,0:T(8,128)S(1)}, u32[]{:S(2)}, u32[]{:S(2)}) collective-permute-start(f32[2,256,512]{2,1,0:T(8,128)S(1)} %get-tuple-element.39), channel_id=1, source_target_pairs={{0,1},{1,0},{2,3},{3,2},{4,5},{5,4},{6,7},{7,6},{8,9},{9,8},{10,11... | collective-permute-start | bytes 3145736 | tf_op jit(solution)/shard_map/ppermute | solution.py:9
  578.9 41.6 %collective-permute-start.8 = (f32[2,256,512]{2,1,0:T(8,128)S(1)}, f32[2,256,512]{2,1,0:T(8,128)S(1)}, u32[]{:S(2)}, u32[]{:S(2)}) collective-permute-start(f32[2,256,512]{2,1,0:T(8,128)S(1)} %get-tuple-element.38), channel_id=1, source_target_pairs={{0,1},{1,0},{2,3},{3,2},{4,5},{5,4},{6,7},{7,6},{8,9},{9,8},{10,11... | collective-permute-start | bytes 3145736 | tf_op jit(solution)/shard_map/ppermute | solution.py:9
  621.1 63.1 %collective-permute-start.10 = (f32[2,256,512]{2,1,0:T(8,128)S(1)}, f32[2,256,512]{2,1,0:T(8,128)S(1)}, u32[]{:S(2)}, u32[]{:S(2)}) collective-permute-start(f32[2,256,512]{2,1,0:T(8,128)S(1)} %get-tuple-element.30), channel_id=1, source_target_pairs={{0,2},{1,3},{2,0},{3,1},{4,6},{5,7},{6,4},{7,5},{8,10},{9,11},{10,... | collective-permute-start | bytes 3145736 | tf_op jit(solution)/shard_map/ppermute | solution.py:9
  622.4 84.3 %collective-permute-start.9 = (f32[2,256,512]{2,1,0:T(8,128)S(1)}, f32[2,256,512]{2,1,0:T(8,128)S(1)}, u32[]{:S(2)}, u32[]{:S(2)}) collective-permute-start(f32[2,256,512]{2,1,0:T(8,128)S(1)} %get-tuple-element.31), channel_id=1, source_target_pairs={{0,2},{1,3},{2,0},{3,1},{4,6},{5,7},{6,4},{7,5},{8,10},{9,11},{10,... | collective-permute-start | bytes 3145736 | tf_op jit(solution)/shard_map/ppermute | solution.py:9
  663.3 180.2 %collective-permute-start.23 = (f32[4,256,512]{2,1,0:T(8,128)S(1)}, f32[4,256,512]{2,1,0:T(8,128)S(1)}, u32[]{:S(2)}, u32[]{:S(2)}) collective-permute-start(f32[4,256,512]{2,1,0:T(8,128)S(1)} %get-tuple-element.9), channel_id=1, source_target_pairs={{0,4},{1,5},{2,6},{3,7},{4,0},{5,1},{6,2},{7,3},{8,12},{9,13},{10,... | collective-permute-start | bytes 6291464 | tf_op jit(solution)/shard_map/ppermute | solution.py:9
  665.1 178.9 %collective-permute-start.24 = (f32[4,256,512]{2,1,0:T(8,128)S(1)}, f32[4,256,512]{2,1,0:T(8,128)S(1)}, u32[]{:S(2)}, u32[]{:S(2)}) collective-permute-start(f32[4,256,512]{2,1,0:T(8,128)S(1)} %get-tuple-element.8), channel_id=1, source_target_pairs={{0,4},{1,5},{2,6},{3,7},{4,0},{5,1},{6,2},{7,3},{8,12},{9,13},{10,... | collective-permute-start | bytes 6291464 | tf_op jit(solution)/shard_map/ppermute | solution.py:9
  707.4 135.0 %copy-start.2 = (f32[3,1,256,512]{3,2,1,0:T(8,128)S(1)}, f32[3,1,256,512]{3,2,1,0:T(8,128)}, u32[]{:S(2)}) copy-start(f32[3,1,256,512]{3,2,1,0:T(8,128)} %copy-done.1) | copy-start | bytes 4718596
  707.4 135.0 %copy-start.17 = (f32[256,512]{1,0:T(8,128)S(1)}, f32[256,512]{1,0:T(8,128)}, u32[]{:S(2)}) copy-start(f32[256,512]{1,0:T(8,128)} %copy-done.16) | copy-start | bytes 1572868
  707.4 135.0 %copy-start.18 = (f32[512]{0:T(512)S(1)}, f32[512]{0:T(512)}, u32[]{:S(2)}) copy-start(f32[512]{0:T(512)} %param.9) | copy-start | bytes 6148
  707.4 112.5 %collective-permute-start.11 = (f32[2,256,512]{2,1,0:T(8,128)S(1)}, f32[2,256,512]{2,1,0:T(8,128)S(1)}, u32[]{:S(2)}, u32[]{:S(2)}) collective-permute-start(f32[2,256,512]{2,1,0:T(8,128)S(1)} %get-tuple-element.28), channel_id=1, source_target_pairs={{0,4},{1,5},{2,6},{3,7},{4,0},{5,1},{6,2},{7,3},{8,12},{9,13},{10,... | collective-permute-start | bytes 3145736 | tf_op jit(solution)/shard_map/ppermute | solution.py:9
  709.2 133.1 %collective-permute-start.12 = (f32[2,256,512]{2,1,0:T(8,128)S(1)}, f32[2,256,512]{2,1,0:T(8,128)S(1)}, u32[]{:S(2)}, u32[]{:S(2)}) collective-permute-start(f32[2,256,512]{2,1,0:T(8,128)S(1)} %get-tuple-element.29), channel_id=1, source_target_pairs={{0,4},{1,5},{2,6},{3,7},{4,0},{5,1},{6,2},{7,3},{8,12},{9,13},{10,... | collective-permute-start | bytes 3145736 | tf_op jit(solution)/shard_map/ppermute | solution.py:9
  845.8 314.3 %all-reduce.7.cloned.1.call-start = ((), (), s32[]{:S(2)}) async-start(), calls=%async_computation.1 | async-start | bytes 16777216 | tf_op jit(solution)/shard_map/psum | solution.py:215
  850.5 1.0 copy-start.9
  852.8 6.5 copy-start.10
  852.8 6.5 collective-permute-start.25
Sparse Core Ops, SparseCore 0:
  845.9 144.8 all-reduce.4
  997.3 162.7 all-reduce.6
where the time goes:
time: 1180 us
  waiting for transfers between devices  990 us (84%)
  matrix products  67.5 us (6%)
  other arithmetic  58.3 us (5%)
  starting transfers between devices  31.8 us (3%)
  between operations  14.8 us (1%)
  local copies, waits for them, and re-layouts  12.9 us (1%)
    ppermute x24, waiting for transfers between devices, swapped(): lax.ppermute(array, axis, [(i, i ^ 1 << apart) for i in range(lax.axis_si...  693 us
    psum x1, waiting for transfers between devices, on_device(): grad_out_weight = lax.psum(partial_value, ('dp', 'seq')) * grad_scale  167 us
    psum x1, waiting for transfers between devices, on_device(): grad_filter = lax.psum(filter_part, 'dp') * grad_scale  130 us
    dot_general x16, matrix products, table_apply(): return jnp.einsum(pattern, matrix, values, precision=lax.Precision.HIGHEST)  56.8 us
    ppermute x24, starting transfers between devices, swapped(): lax.ppermute(array, axis, [(i, i ^ 1 << apart) for i in range(lax.axis_si...  26 us
  transfers between devices with their start and end apart: 28, of which 21 were waited for; matrix products, arithmetic and copies ran while one was open for 6% of the time, Pallas kernels for 0%

commit v1 on v0

--- a/solution.py
+++ b/solution.py
@@ -213,7 +213,7 @@
         mixed_flat, grad_flat, (((0,), (0,)), ((), ())), preferred_element_type=jnp.float32
     )
     grad_out_weight = lax.psum(partial_value, ("dp", "seq")) * grad_scale
-    grad_filter = lax.psum(filter_part, "dp") * grad_scale
+    grad_filter = jnp.sum(lax.all_gather(filter_part, "dp"), axis=0) * grad_scale
     return (layer_out, grad_streams.astype(jnp.bfloat16), grad_filter, grad_out_weight)
 
 

time: 1180 us -> 1080 us (0.915)
  waiting for transfers between devices: 990 us -> 882 us
    psum x1 -> x0, waiting for transfers between devices: 130 us -> none  [on_device(): grad_filter = lax.psum(filter_part, 'dp') * grad_scale]
    psum x1, waiting for transfers between devices: 167 us -> 187 us  [on_device(): grad_out_weight = lax.psum(partial_value, ('dp', 'seq')) * grad_scale]
  transfers between devices with their start and end apart: 28 -> 28, of which waited for: 21 -> 20; matrix products, arithmetic and copies ran while one was open for 6% -> 6% of each run, Pallas kernels for 0% -> 0%
where the time goes in v1:
time: 1080 us; the launch traced here: 1070 us
  waiting for transfers between devices  882 us (82%)
  matrix products  70.1 us (6%)
  other arithmetic  60.2 us (6%)
  starting transfers between devices  31.3 us (3%)
  between operations  16.3 us (2%)
  local copies, waits for them, and re-layouts  13.1 us (1%)
    ppermute x24, waiting for transfers between devices, swapped(): lax.ppermute(array, axis, [(i, i ^ 1 << apart) for i in range(lax.axis_si...  695 us
    psum x1, waiting for transfers between devices, on_device(): grad_out_weight = lax.psum(partial_value, ('dp', 'seq')) * grad_scale  187 us
    dot_general x16, matrix products, table_apply(): return jnp.einsum(pattern, matrix, values, precision=lax.Precision.HIGHEST)  59.4 us
    ppermute x24, starting transfers between devices, swapped(): lax.ppermute(array, axis, [(i, i ^ 1 << apart) for i in range(lax.axis_si...  25.7 us
  transfers between devices with their start and end apart: 28, of which 20 were waited for; matrix products, arithmetic and copies ran while one was open for 6% of the time, Pallas kernels for 0%

profile of v1, /device:TPU:1, one launch (start us, length us, event | category | flops | bytes accessed | tf_op | source)
XLA Modules:
  0.0 1072.9 jit_solution(11540240948079647801)
XLA Ops:
  8.9 4.0 collective-permute-start
  14.0 1.4 maximum_convert_fusion
  16.7 1.5 pad_maximum_fusion
  18.8 1.6 concatenate.47
  20.4 3.8 collective-permute-start.2
  26.8 2.9 collective-permute-start.14
  31.8 36.8 %collective-permute-done.2 = f32[4,256,512]{2,1,0:T(8,128)} collective-permute-done((f32[4,256,512]{2,1,0:T(8,128)}, f32[4,256,512]{2,1,0:T(8,128)}, u32[]{:S(2)}, u32[]{:S(2)}) %collective-permute-start.2) | collective-permute-done | bytes 2097184 | tf_op jit(solution)/shard_map/ppermute | solution.py:9
  68.6 44.9 %collective-permute-done.1 = f32[4,256,512]{2,1,0:T(8,128)} collective-permute-done((f32[4,256,512]{2,1,0:T(8,128)}, f32[4,256,512]{2,1,0:T(8,128)}, u32[]{:S(2)}, u32[]{:S(2)}) %collective-permute-start.1) | collective-permute-done | bytes 2097184 | tf_op jit(solution)/shard_map/ppermute | solution.py:9
  113.6 6.2 add_select_fusion.9
  121.2 14.8 %collective-permute-done.14 = f32[2,256,512]{2,1,0:T(8,128)} collective-permute-done((f32[2,256,512]{2,1,0:T(8,128)}, f32[2,256,512]{2,1,0:T(8,128)}, u32[]{:S(2)}, u32[]{:S(2)}) %collective-permute-start.14) | collective-permute-done | bytes 1048608 | tf_op jit(solution)/shard_map/ppermute | solution.py:9
  136.0 22.5 %collective-permute-done.13 = f32[2,256,512]{2,1,0:T(8,128)} collective-permute-done((f32[2,256,512]{2,1,0:T(8,128)}, f32[2,256,512]{2,1,0:T(8,128)}, u32[]{:S(2)}, u32[]{:S(2)}) %collective-permute-start.13) | collective-permute-done | bytes 1048608 | tf_op jit(solution)/shard_map/ppermute | solution.py:9
  158.5 3.4 add_select_fusion.14
  163.4 107.4 %collective-permute-done.16 = f32[2,256,512]{2,1,0:T(8,128)} collective-permute-done((f32[2,256,512]{2,1,0:T(8,128)}, f32[2,256,512]{2,1,0:T(8,128)}, u32[]{:S(2)}, u32[]{:S(2)}) %collective-permute-start.16) | collective-permute-done | bytes 1048608 | tf_op jit(solution)/shard_map/ppermute | solution.py:9
  270.9 22.5 %collective-permute-done.15 = f32[2,256,512]{2,1,0:T(8,128)} collective-permute-done((f32[2,256,512]{2,1,0:T(8,128)}, f32[2,256,512]{2,1,0:T(8,128)}, u32[]{:S(2)}, u32[]{:S(2)}) %collective-permute-start.15) | collective-permute-done | bytes 1048608 | tf_op jit(solution)/shard_map/ppermute | solution.py:9
  293.3 4.1 add_select_fusion.12
  298.9 6.7 add_select_fusion.7
  306.0 1.5 collective-permute-start.6
  307.6 12.1 %collective-permute-done.18 = f32[2,256,512]{2,1,0:T(8,128)} collective-permute-done((f32[2,256,512]{2,1,0:T(8,128)}, f32[2,256,512]{2,1,0:T(8,128)}, u32[]{:S(2)}, u32[]{:S(2)}) %collective-permute-start.18) | collective-permute-done | bytes 1048608 | tf_op jit(solution)/shard_map/ppermute | solution.py:9
  319.7 22.5 %collective-permute-done.17 = f32[2,256,512]{2,1,0:T(8,128)} collective-permute-done((f32[2,256,512]{2,1,0:T(8,128)}, f32[2,256,512]{2,1,0:T(8,128)}, u32[]{:S(2)}, u32[]{:S(2)}) %collective-permute-start.17) | collective-permute-done | bytes 1048608 | tf_op jit(solution)/shard_map/ppermute | solution.py:9
  342.1 2.7 add_select_fusion.10
  344.9 2.7 convolution_multiply_fusion
  347.5 2.7 fusion.10
  350.2 2.7 convolution_multiply_fusion.1
  352.9 34.2 %collective-permute-done.5 = f32[4,256,512]{2,1,0:T(8,128)} collective-permute-done((f32[4,256,512]{2,1,0:T(8,128)}, f32[4,256,512]{2,1,0:T(8,128)}, u32[]{:S(2)}, u32[]{:S(2)}) %collective-permute-start.5) | collective-permute-done | bytes 2097184 | tf_op jit(solution)/shard_map/ppermute | solution.py:9
  387.1 44.9 %collective-permute-done.6 = f32[4,256,512]{2,1,0:T(8,128)} collective-permute-done((f32[4,256,512]{2,1,0:T(8,128)}, f32[4,256,512]{2,1,0:T(8,128)}, u32[]{:S(2)}, u32[]{:S(2)}) %collective-permute-start.6) | collective-permute-done | bytes 2097184 | tf_op jit(solution)/shard_map/ppermute | solution.py:9
  432.0 4.6 add_select_fusion.5
  436.7 4.7 fusion.39
  441.4 4.5 fusion.41
  445.9 4.5 multiply_add_fusion
  450.4 4.7 multiply_subtract_fusion
  455.1 6.3 multiply_subtract_fusion.2
  461.4 1.5 pad_maximum_fusion.2
  462.9 2.9 copy.61
  465.8 6.1 fusion.43
  471.9 1.5 pad_maximum_fusion.1
  473.4 3.3 copy.60
  476.7 4.8 fusion.45
  481.5 3.3 convolution_add_fusion
  484.8 3.8 select_bitcast_fusion
  490.4 2.1 fusion.15
  492.5 2.1 fusion.19
  494.6 2.1 convolution_add_fusion.2
  496.7 35.5 %collective-permute-done.20 = f32[4,256,512]{2,1,0:T(8,128)S(1)} collective-permute-done((f32[4,256,512]{2,1,0:T(8,128)S(1)}, f32[4,256,512]{2,1,0:T(8,128)S(1)}, u32[]{:S(2)}, u32[]{:S(2)}) %collective-permute-start.20) | collective-permute-done | bytes 2097184 | tf_op jit(solution)/shard_map/ppermute | solution.py:9
  532.2 44.9 %collective-permute-done.19 = f32[4,256,512]{2,1,0:T(8,128)S(1)} collective-permute-done((f32[4,256,512]{2,1,0:T(8,128)S(1)}, f32[4,256,512]{2,1,0:T(8,128)S(1)}, u32[]{:S(2)}, u32[]{:S(2)}) %collective-permute-start.19) | collective-permute-done | bytes 2097184 | tf_op jit(solution)/shard_map/ppermute | solution.py:9
  577.1 1.5 multiply_select_fusion.2
  580.1 2.5 select_bitcast_fusion.2
  584.2 18.0 %collective-permute-done.8 = f32[2,256,512]{2,1,0:T(8,128)S(1)} collective-permute-done((f32[2,256,512]{2,1,0:T(8,128)S(1)}, f32[2,256,512]{2,1,0:T(8,128)S(1)}, u32[]{:S(2)}, u32[]{:S(2)}) %collective-permute-start.8) | collective-permute-done | bytes 1048608 | tf_op jit(solution)/shard_map/ppermute | solution.py:9
  602.2 22.5 %collective-permute-done.7 = f32[2,256,512]{2,1,0:T(8,128)S(1)} collective-permute-done((f32[2,256,512]{2,1,0:T(8,128)S(1)}, f32[2,256,512]{2,1,0:T(8,128)S(1)}, u32[]{:S(2)}, u32[]{:S(2)}) %collective-permute-start.7) | collective-permute-done | bytes 1048608 | tf_op jit(solution)/shard_map/ppermute | solution.py:9
  625.3 1.5 collective-permute-start.10
  627.1 39.0 %collective-permute-done.21 = f32[4,256,512]{2,1,0:T(8,128)S(1)} collective-permute-done((f32[4,256,512]{2,1,0:T(8,128)S(1)}, f32[4,256,512]{2,1,0:T(8,128)S(1)}, u32[]{:S(2)}, u32[]{:S(2)}) %collective-permute-start.21) | collective-permute-done | bytes 2097184 | tf_op jit(solution)/shard_map/ppermute | solution.py:9
  666.2 1.5 multiply_select_fusion
  667.6 1.8 collective-permute-start.23
  670.7 17.9 %collective-permute-done.10 = f32[2,256,512]{2,1,0:T(8,128)S(1)} collective-permute-done((f32[2,256,512]{2,1,0:T(8,128)S(1)}, f32[2,256,512]{2,1,0:T(8,128)S(1)}, u32[]{:S(2)}, u32[]{:S(2)}) %collective-permute-start.10) | collective-permute-done | bytes 1048608 | tf_op jit(solution)/shard_map/ppermute | solution.py:9
  688.6 22.5 %collective-permute-done.9 = f32[2,256,512]{2,1,0:T(8,128)S(1)} collective-permute-done((f32[2,256,512]{2,1,0:T(8,128)S(1)}, f32[2,256,512]{2,1,0:T(8,128)S(1)}, u32[]{:S(2)}, u32[]{:S(2)}) %collective-permute-start.9) | collective-permute-done | bytes 1048608 | tf_op jit(solution)/shard_map/ppermute | solution.py:9
  711.8 1.8 collective-permute-start.11
  714.9 109.4 %collective-permute-done.11 = f32[2,256,512]{2,1,0:T(8,128)S(1)} collective-permute-done((f32[2,256,512]{2,1,0:T(8,128)S(1)}, f32[2,256,512]{2,1,0:T(8,128)S(1)}, u32[]{:S(2)}, u32[]{:S(2)}) %collective-permute-start.11) | collective-permute-done | bytes 1048608 | tf_op jit(solution)/shard_map/ppermute | solution.py:9
  824.5 22.2 %collective-permute-done.12 = f32[2,256,512]{2,1,0:T(8,128)S(1)} collective-permute-done((f32[2,256,512]{2,1,0:T(8,128)S(1)}, f32[2,256,512]{2,1,0:T(8,128)S(1)}, u32[]{:S(2)}, u32[]{:S(2)}) %collective-permute-start.12) | collective-permute-done | bytes 1048608 | tf_op jit(solution)/shard_map/ppermute | solution.py:9
  850.1 4.7 fusion.1
  857.0 1.4 collective-permute-start.25
  858.5 4.8 fusion
  863.4 1.4 fusion.6
  864.8 186.9 %all-reduce.4.cloned.1.call-done = f32[512,4096]{1,0:T(8,128)} async-done(((f32[512,4096]{1,0:T(8,128)}), f32[512,4096]{1,0:T(8,128)}) %all-reduce.4.cloned.1.call-update) | async-done | bytes 8388624 | tf_op jit(solution)/shard_map/psum | solution.py:215
  1051.7 8.3 broadcast_multiply_fusion
  1060.0 4.4 reduce_sum.8
  (107 shorter events, 29.1 us)
Async XLA Ops:
  8.0 16.2 %copy-start = (bf16[1,256,4096]{2,1,0:T(8,128)(2,1)S(1)}, bf16[1,256,4096]{2,1,0:T(8,128)(2,1)}, u32[]{:S(2)}) copy-start(bf16[1,256,4096]{2,1,0:T(8,128)(2,1)} %param.11) | copy-start | bytes 6291460
  8.0 1043.7 %all-reduce.4.cloned.1.call-start = ((), (), s32[]{:S(2)}) async-start(), calls=%async_computation.1 | async-start | bytes 16777216 | tf_op jit(solution)/shard_map/psum | solution.py:215
  8.9 5.0 collective-permute-start
  15.4 1.0 copy-start.12
  15.9 9.7 copy-start.1
  16.7 1.7 copy-start.6
  16.7 2.1 copy-start.5
  16.7 7.5 copy-start.22
  20.4 48.2 %collective-permute-start.2 = (f32[4,256,512]{2,1,0:T(8,128)}, f32[4,256,512]{2,1,0:T(8,128)}, u32[]{:S(2)}, u32[]{:S(2)}) collective-permute-start(f32[4,256,512]{2,1,0:T(8,128)} %concatenate.47), channel_id=1, source_target_pairs={{0,4},{1,5},{2,6},{3,7},{4,0},{5,1},{6,2},{7,3},{8,12},{9,13},{10,... | collective-permute-start | bytes 6291464 | tf_op jit(solution)/shard_map/ppermute | solution.py:9
  24.2 89.4 %collective-permute-start.1 = (f32[4,256,512]{2,1,0:T(8,128)}, f32[4,256,512]{2,1,0:T(8,128)}, u32[]{:S(2)}, u32[]{:S(2)}) collective-permute-start(f32[4,256,512]{2,1,0:T(8,128)} %pad_maximum_fusion), channel_id=1, source_target_pairs={{0,4},{1,5},{2,6},{3,7},{4,0},{5,1},{6,2},{7,3},{8,12},{9,13},{10,... | collective-permute-start | bytes 6291464 | tf_op jit(solution)/shard_map/ppermute | solution.py:9
  25.5 4.4 copy-start.19
  25.6 4.1 copy-start.15
  26.8 109.2 %collective-permute-start.14 = (f32[2,256,512]{2,1,0:T(8,128)}, f32[2,256,512]{2,1,0:T(8,128)}, u32[]{:S(2)}, u32[]{:S(2)}) collective-permute-start(f32[2,256,512]{2,1,0:T(8,128)} %concatenate.49), channel_id=1, source_target_pairs={{0,4},{1,5},{2,6},{3,7},{4,0},{5,1},{6,2},{7,3},{8,12},{9,13},{10,... | collective-permute-start | bytes 3145736 | tf_op jit(solution)/shard_map/ppermute | solution.py:9
  29.9 0.8 copy-start.13
  31.7 126.7 %collective-permute-start.13 = (f32[2,256,512]{2,1,0:T(8,128)}, f32[2,256,512]{2,1,0:T(8,128)}, u32[]{:S(2)}, u32[]{:S(2)}) collective-permute-start(f32[2,256,512]{2,1,0:T(8,128)} %pad_maximum_fusion.6), channel_id=1, source_target_pairs={{0,4},{1,5},{2,6},{3,7},{4,0},{5,1},{6,2},{7,3},{8,12},{9,13},{10,... | collective-permute-start | bytes 3145736 | tf_op jit(solution)/shard_map/ppermute | solution.py:9
  113.5 44.9 %copy-start.14 = (f32[1,256,512]{2,1,0:T(8,128)S(1)}, f32[1,256,512]{2,1,0:T(8,128)}, u32[]{:S(2)}) copy-start(f32[1,256,512]{2,1,0:T(8,128)} %copy-done.13) | copy-start | bytes 1572868
  113.5 44.9 %copy-start.16 = (f32[1,256,512]{2,1,0:T(8,128)S(1)}, f32[1,256,512]{2,1,0:T(8,128)}, u32[]{:S(2)}) copy-start(f32[1,256,512]{2,1,0:T(8,128)} %copy-done.15) | copy-start | bytes 1572868
  119.8 179.2 %collective-permute-start.3 = (f32[4,256,512]{2,1,0:T(8,128)}, f32[4,256,512]{2,1,0:T(8,128)}, u32[]{:S(2)}, u32[]{:S(2)}) collective-permute-start(f32[4,256,512]{2,1,0:T(8,128)} %get-tuple-element.16), channel_id=1, source_target_pairs={{0,2},{1,3},{2,0},{3,1},{4,6},{5,7},{6,4},{7,5},{8,10},{9,11},{10,... | collective-permute-start | bytes 6291464 | tf_op jit(solution)/shard_map/ppermute | solution.py:9
  120.9 178.0 %collective-permute-start.4 = (f32[4,256,512]{2,1,0:T(8,128)}, f32[4,256,512]{2,1,0:T(8,128)}, u32[]{:S(2)}, u32[]{:S(2)}) collective-permute-start(f32[4,256,512]{2,1,0:T(8,128)} %get-tuple-element.17), channel_id=1, source_target_pairs={{0,2},{1,3},{2,0},{3,1},{4,6},{5,7},{6,4},{7,5},{8,10},{9,11},{10,... | collective-permute-start | bytes 6291464 | tf_op jit(solution)/shard_map/ppermute | solution.py:9
  161.9 109.0 %collective-permute-start.16 = (f32[2,256,512]{2,1,0:T(8,128)}, f32[2,256,512]{2,1,0:T(8,128)}, u32[]{:S(2)}, u32[]{:S(2)}) collective-permute-start(f32[2,256,512]{2,1,0:T(8,128)} %get-tuple-element.34), channel_id=1, source_target_pairs={{0,2},{1,3},{2,0},{3,1},{4,6},{5,7},{6,4},{7,5},{8,10},{9,11},{10,... | collective-permute-start | bytes 3145736 | tf_op jit(solution)/shard_map/ppermute | solution.py:9
  163.1 130.3 %collective-permute-start.15 = (f32[2,256,512]{2,1,0:T(8,128)}, f32[2,256,512]{2,1,0:T(8,128)}, u32[]{:S(2)}, u32[]{:S(2)}) collective-permute-start(f32[2,256,512]{2,1,0:T(8,128)} %get-tuple-element.35), channel_id=1, source_target_pairs={{0,2},{1,3},{2,0},{3,1},{4,6},{5,7},{6,4},{7,5},{8,10},{9,11},{10,... | collective-permute-start | bytes 3145736 | tf_op jit(solution)/shard_map/ppermute | solution.py:9
  297.5 22.2 %collective-permute-start.18 = (f32[2,256,512]{2,1,0:T(8,128)}, f32[2,256,512]{2,1,0:T(8,128)}, u32[]{:S(2)}, u32[]{:S(2)}) collective-permute-start(f32[2,256,512]{2,1,0:T(8,128)} %get-tuple-element.26), channel_id=1, source_target_pairs={{0,1},{1,0},{2,3},{3,2},{4,5},{5,4},{6,7},{7,6},{8,9},{9,8},{10,11... | collective-permute-start | bytes 3145736 | tf_op jit(solution)/shard_map/ppermute | solution.py:9
  297.9 44.3 %collective-permute-start.17 = (f32[2,256,512]{2,1,0:T(8,128)}, f32[2,256,512]{2,1,0:T(8,128)}, u32[]{:S(2)}, u32[]{:S(2)}) collective-permute-start(f32[2,256,512]{2,1,0:T(8,128)} %get-tuple-element.27), channel_id=1, source_target_pairs={{0,1},{1,0},{2,3},{3,2},{4,5},{5,4},{6,7},{7,6},{8,9},{9,8},{10,11... | collective-permute-start | bytes 3145736 | tf_op jit(solution)/shard_map/ppermute | solution.py:9
  305.6 81.5 %collective-permute-start.5 = (f32[4,256,512]{2,1,0:T(8,128)}, f32[4,256,512]{2,1,0:T(8,128)}, u32[]{:S(2)}, u32[]{:S(2)}) collective-permute-start(f32[4,256,512]{2,1,0:T(8,128)} %get-tuple-element.14), channel_id=1, source_target_pairs={{0,1},{1,0},{2,3},{3,2},{4,5},{5,4},{6,7},{7,6},{8,9},{9,8},{10,11... | collective-permute-start | bytes 6291464 | tf_op jit(solution)/shard_map/ppermute | solution.py:9
  306.0 126.0 %collective-permute-start.6 = (f32[4,256,512]{2,1,0:T(8,128)}, f32[4,256,512]{2,1,0:T(8,128)}, u32[]{:S(2)}, u32[]{:S(2)}) collective-permute-start(f32[4,256,512]{2,1,0:T(8,128)} %get-tuple-element.15), channel_id=1, source_target_pairs={{0,1},{1,0},{2,3},{3,2},{4,5},{5,4},{6,7},{7,6},{8,9},{9,8},{10,11... | collective-permute-start | bytes 6291464 | tf_op jit(solution)/shard_map/ppermute | solution.py:9
  465.8 6.1 copy-start.17
  465.8 6.1 copy-start.18
  476.6 4.8 copy-start.3
  476.7 4.8 copy-start.9
  481.5 3.3 copy-start.4
  484.8 5.6 copy-start.7
  488.6 3.8 copy-start.8
  488.6 43.5 %collective-permute-start.20 = (f32[4,256,512]{2,1,0:T(8,128)S(1)}, f32[4,256,512]{2,1,0:T(8,128)S(1)}, u32[]{:S(2)}, u32[]{:S(2)}) collective-permute-start(f32[4,256,512]{2,1,0:T(8,128)S(1)} %get-tuple-element.22), channel_id=1, source_target_pairs={{0,1},{1,0},{2,3},{3,2},{4,5},{5,4},{6,7},{7,6},{8,9},{9,8},{10,11... | collective-permute-start | bytes 6291464 | tf_op jit(solution)/shard_map/ppermute | solution.py:9
  489.1 88.0 %collective-permute-start.19 = (f32[4,256,512]{2,1,0:T(8,128)S(1)}, f32[4,256,512]{2,1,0:T(8,128)S(1)}, u32[]{:S(2)}, u32[]{:S(2)}) collective-permute-start(f32[4,256,512]{2,1,0:T(8,128)S(1)} %get-tuple-element.23), channel_id=1, source_target_pairs={{0,1},{1,0},{2,3},{3,2},{4,5},{5,4},{6,7},{7,6},{8,9},{9,8},{10,11... | collective-permute-start | bytes 6291464 | tf_op jit(solution)/shard_map/ppermute | solution.py:9
  578.6 48.5 %collective-permute-start.22 = (f32[4,256,512]{2,1,0:T(8,128)S(1)}, f32[4,256,512]{2,1,0:T(8,128)S(1)}, u32[]{:S(2)}, u32[]{:S(2)}) collective-permute-start(f32[4,256,512]{2,1,0:T(8,128)S(1)} %get-tuple-element.10), channel_id=1, source_target_pairs={{0,2},{1,3},{2,0},{3,1},{4,6},{5,7},{6,4},{7,5},{8,10},{9,11},{10,... | collective-permute-start | bytes 6291464 | tf_op jit(solution)/shard_map/ppermute | solution.py:9
  579.9 86.3 %collective-permute-start.21 = (f32[4,256,512]{2,1,0:T(8,128)S(1)}, f32[4,256,512]{2,1,0:T(8,128)S(1)}, u32[]{:S(2)}, u32[]{:S(2)}) collective-permute-start(f32[4,256,512]{2,1,0:T(8,128)S(1)} %get-tuple-element.11), channel_id=1, source_target_pairs={{0,2},{1,3},{2,0},{3,1},{4,6},{5,7},{6,4},{7,5},{8,10},{9,11},{10,... | collective-permute-start | bytes 6291464 | tf_op jit(solution)/shard_map/ppermute | solution.py:9
  582.6 19.6 %collective-permute-start.8 = (f32[2,256,512]{2,1,0:T(8,128)S(1)}, f32[2,256,512]{2,1,0:T(8,128)S(1)}, u32[]{:S(2)}, u32[]{:S(2)}) collective-permute-start(f32[2,256,512]{2,1,0:T(8,128)S(1)} %get-tuple-element.38), channel_id=1, source_target_pairs={{0,1},{1,0},{2,3},{3,2},{4,5},{5,4},{6,7},{7,6},{8,9},{9,8},{10,11... | collective-permute-start | bytes 3145736 | tf_op jit(solution)/shard_map/ppermute | solution.py:9
  583.1 41.6 %collective-permute-start.7 = (f32[2,256,512]{2,1,0:T(8,128)S(1)}, f32[2,256,512]{2,1,0:T(8,128)S(1)}, u32[]{:S(2)}, u32[]{:S(2)}) collective-permute-start(f32[2,256,512]{2,1,0:T(8,128)S(1)} %get-tuple-element.39), channel_id=1, source_target_pairs={{0,1},{1,0},{2,3},{3,2},{4,5},{5,4},{6,7},{7,6},{8,9},{9,8},{10,11... | collective-permute-start | bytes 3145736 | tf_op jit(solution)/shard_map/ppermute | solution.py:9
  625.3 63.3 %collective-permute-start.10 = (f32[2,256,512]{2,1,0:T(8,128)S(1)}, f32[2,256,512]{2,1,0:T(8,128)S(1)}, u32[]{:S(2)}, u32[]{:S(2)}) collective-permute-start(f32[2,256,512]{2,1,0:T(8,128)S(1)} %get-tuple-element.30), channel_id=1, source_target_pairs={{0,2},{1,3},{2,0},{3,1},{4,6},{5,7},{6,4},{7,5},{8,10},{9,11},{10,... | collective-permute-start | bytes 3145736 | tf_op jit(solution)/shard_map/ppermute | solution.py:9
  626.8 84.3 %collective-permute-start.9 = (f32[2,256,512]{2,1,0:T(8,128)S(1)}, f32[2,256,512]{2,1,0:T(8,128)S(1)}, u32[]{:S(2)}, u32[]{:S(2)}) collective-permute-start(f32[2,256,512]{2,1,0:T(8,128)S(1)} %get-tuple-element.31), channel_id=1, source_target_pairs={{0,2},{1,3},{2,0},{3,1},{4,6},{5,7},{6,4},{7,5},{8,10},{9,11},{10,... | collective-permute-start | bytes 3145736 | tf_op jit(solution)/shard_map/ppermute | solution.py:9
  667.6 180.2 %collective-permute-start.23 = (f32[4,256,512]{2,1,0:T(8,128)S(1)}, f32[4,256,512]{2,1,0:T(8,128)S(1)}, u32[]{:S(2)}, u32[]{:S(2)}) collective-permute-start(f32[4,256,512]{2,1,0:T(8,128)S(1)} %get-tuple-element.9), channel_id=1, source_target_pairs={{0,4},{1,5},{2,6},{3,7},{4,0},{5,1},{6,2},{7,3},{8,12},{9,13},{10,... | collective-permute-start | bytes 6291464 | tf_op jit(solution)/shard_map/ppermute | solution.py:9
  669.5 178.9 %collective-permute-start.24 = (f32[4,256,512]{2,1,0:T(8,128)S(1)}, f32[4,256,512]{2,1,0:T(8,128)S(1)}, u32[]{:S(2)}, u32[]{:S(2)}) collective-permute-start(f32[4,256,512]{2,1,0:T(8,128)S(1)} %get-tuple-element.8), channel_id=1, source_target_pairs={{0,4},{1,5},{2,6},{3,7},{4,0},{5,1},{6,2},{7,3},{8,12},{9,13},{10,... | collective-permute-start | bytes 6291464 | tf_op jit(solution)/shard_map/ppermute | solution.py:9
  711.8 135.0 %copy-start.2 = (f32[3,1,256,512]{3,2,1,0:T(8,128)S(1)}, f32[3,1,256,512]{3,2,1,0:T(8,128)}, u32[]{:S(2)}) copy-start(f32[3,1,256,512]{3,2,1,0:T(8,128)} %copy-done.1) | copy-start | bytes 4718596
  711.8 135.0 %copy-start.20 = (f32[256,512]{1,0:T(8,128)S(1)}, f32[256,512]{1,0:T(8,128)}, u32[]{:S(2)}) copy-start(f32[256,512]{1,0:T(8,128)} %copy-done.19) | copy-start | bytes 1572868
  711.8 134.9 %copy-start.21 = (f32[512]{0:T(512)S(1)}, f32[512]{0:T(512)}, u32[]{:S(2)}) copy-start(f32[512]{0:T(512)} %param.9) | copy-start | bytes 6148
  711.8 112.5 %collective-permute-start.11 = (f32[2,256,512]{2,1,0:T(8,128)S(1)}, f32[2,256,512]{2,1,0:T(8,128)S(1)}, u32[]{:S(2)}, u32[]{:S(2)}) collective-permute-start(f32[2,256,512]{2,1,0:T(8,128)S(1)} %get-tuple-element.28), channel_id=1, source_target_pairs={{0,4},{1,5},{2,6},{3,7},{4,0},{5,1},{6,2},{7,3},{8,12},{9,13},{10,... | collective-permute-start | bytes 3145736 | tf_op jit(solution)/shard_map/ppermute | solution.py:9
  713.6 133.1 %collective-permute-start.12 = (f32[2,256,512]{2,1,0:T(8,128)S(1)}, f32[2,256,512]{2,1,0:T(8,128)S(1)}, u32[]{:S(2)}, u32[]{:S(2)}) collective-permute-start(f32[2,256,512]{2,1,0:T(8,128)S(1)} %get-tuple-element.29), channel_id=1, source_target_pairs={{0,4},{1,5},{2,6},{3,7},{4,0},{5,1},{6,2},{7,3},{8,12},{9,13},{10,... | collective-permute-start | bytes 3145736 | tf_op jit(solution)/shard_map/ppermute | solution.py:9
  854.8 1.0 copy-start.10
  854.8 205.1 %all-gather.2.cloned.1.call-start = ((), (), s32[]{:S(2)}) async-start(), calls=%async_computation | async-start | bytes 8912896 | tf_op jit(solution)/shard_map/all_gather | solution.py:216
  857.0 6.2 copy-start.11
  857.0 6.2 collective-permute-start.25
Sparse Core Ops, SparseCore 0:
  854.9 196.7 all-reduce.3
Sparse Core Ops, SparseCore 1:
  857.8 80.6 all-gather.1
